TPU v7x, 32 devices: a whole 2x2x4 slice. The times are simulated.
32 devices in a mesh: space: 8 (over y, x, core), vz: 4 (over z).
Axes of the slice: x: 2, y: 2, z: 4, core: 2. Of those that a mesh axis runs over, the one named last changes fastest.
Arguments:
- distribution: float32 [48, 16, 8, 2304], P('vz', 'space'), may hold values from 0 to 6, as said below
- collision_rate: float32 [16, 8], P('space'), may hold values from 0.5 to 2
Outputs:
- new_distribution: float32 [48, 16, 8, 2304], P('vz', 'space')
Inputs may be any that keep to these rules, and one draw needn't show every extreme that they name: `distribution`: every entry is positive.
All inputs are finite; a program needn't handle non-finite values.
Results may differ from a plain program's by a relative error of at most 0.000056.
Values sent between devices are 32-bit elements; how exact they have to be, the bound alone decides.
A program may use at most 64 MiB of HBM per device.

v0:
```python
import jax
import jax.numpy as jnp
from jax import lax
from jax.sharding import PartitionSpec as P

V = 48
SWEEPS = 3


vel_max = 4.5
step_ratio = 0.1
collision_scale = 0.004
relax_scale = 0.5


def with_halo(block, sides, width, periodic):
    for axis, dim in sides:
        count = lax.axis_size(axis)
        forward = [(i, i + 1) for i in range(count - 1)]
        if periodic:
            forward.append((count - 1, 0))
        backward = [(target, source) for source, target in forward]
        low = lax.ppermute(
            lax.slice_in_dim(block, block.shape[dim] - width, None, axis=dim), axis, forward
        )
        high = lax.ppermute(lax.slice_in_dim(block, 0, width, axis=dim), axis, backward)
        block = jnp.concatenate([low, block, high], axis=dim)
    return block


def grid_speeds(position):
    return vel_max * (2.0 * position + 1.0 - V) / V


def velocity_columns():
    grid_values = grid_speeds(jnp.arange(V, dtype=jnp.float32))
    return (jnp.repeat(grid_values, V), jnp.tile(grid_values, V))


def beam_warming(middle, near_cells, far_cells, magnitude):
    return (
        middle
        - 0.5 * magnitude * (3.0 * middle - 4.0 * near_cells + far_cells)
        + 0.5 * magnitude * magnitude * (middle - 2.0 * near_cells + far_cells)
    )


def roll_transport(field_data, speed_cols, axis_id):
    positive = speed_cols > 0
    near_cells = jnp.where(
        positive, jnp.roll(field_data, 1, axis_id), jnp.roll(field_data, -1, axis_id)
    )
    far_cells = jnp.where(
        positive, jnp.roll(field_data, 2, axis_id), jnp.roll(field_data, -2, axis_id)
    )
    return beam_warming(field_data, near_cells, far_cells, step_ratio * jnp.abs(speed_cols))


def combine_planes(partial_value, vertical_speeds):
    zero_moment = partial_value[0]
    return jnp.stack(
        [
            jnp.sum(zero_moment, 0),
            jnp.sum(partial_value[1], 0),
            jnp.sum(partial_value[2], 0),
            jnp.sum(vertical_speeds * zero_moment, 0),
            jnp.sum(partial_value[3] + vertical_speeds * vertical_speeds * zero_moment, 0),
        ]
    )


def cell_state(moment_totals):
    grid_spacing = 2.0 * vel_max / V
    unnormalised_mass = moment_totals[0]
    drift_velocity_x = moment_totals[1] / unnormalised_mass
    drift_velocity_y = moment_totals[2] / unnormalised_mass
    drift_velocity_z = moment_totals[3] / unnormalised_mass
    thermal_energy = (
        moment_totals[4] / unnormalised_mass
        - drift_velocity_x * drift_velocity_x
        - drift_velocity_y * drift_velocity_y
        - drift_velocity_z * drift_velocity_z
    ) / 3.0
    return (
        unnormalised_mass * grid_spacing**3,
        drift_velocity_x,
        drift_velocity_y,
        drift_velocity_z,
        thermal_energy,
    )


def maxwellian(cell_entries, velocity_x_grid, velocity_y_grid, vertical_speeds):
    mass_density, drift_velocity_x, drift_velocity_y, drift_velocity_z, thermal_energy = (
        cell_entries
    )
    squared_spread = (
        (velocity_x_grid - drift_velocity_x) ** 2
        + (velocity_y_grid - drift_velocity_y) ** 2
        + (vertical_speeds - drift_velocity_z) ** 2
    )
    return (
        mass_density
        * (2.0 * jnp.pi * thermal_energy) ** (-1.5)
        * jnp.exp(-squared_spread / (2.0 * thermal_energy))
    )


def velocity_shifts(middle):
    zero_row = jnp.zeros(middle.shape[:-1] + (V,), middle.dtype)
    zero_one = jnp.zeros(middle.shape[:-1] + (1,), middle.dtype)
    upper_x_neighbour = jnp.concatenate([middle[..., V:], zero_row], axis=-1)
    lower_x_neighbour = jnp.concatenate([zero_row, middle[..., :-V]], axis=-1)
    upper_y_neighbour = jnp.concatenate([middle[..., 1:], zero_one], axis=-1)
    lower_y_neighbour = jnp.concatenate([zero_one, middle[..., :-1]], axis=-1)
    return (upper_x_neighbour, lower_x_neighbour, upper_y_neighbour, lower_y_neighbour)


def relaxation_pass(
    bordered_grid,
    forcing_term,
    diagonal_factor,
    vertical_speeds,
    cell_entries,
    collide_rate,
    velocity_x_grid,
    velocity_y_grid,
    upper_mask,
    lower_mask,
):
    mass_density, drift_velocity_x, drift_velocity_y, drift_velocity_z, thermal_energy = (
        cell_entries
    )
    grid_spacing = 2.0 * vel_max / V
    stiffness_factor = thermal_energy / (grid_spacing * grid_spacing)
    half_timestep = 0.5 / grid_spacing
    middle = bordered_grid[1:-1]
    upper_x_neighbour, lower_x_neighbour, upper_y_neighbour, lower_y_neighbour = velocity_shifts(
        middle
    )
    running_total = forcing_term + collide_rate * (
        (stiffness_factor + (velocity_x_grid + grid_spacing - drift_velocity_x) * half_timestep)
        * upper_x_neighbour
        + (stiffness_factor - (velocity_x_grid - grid_spacing - drift_velocity_x) * half_timestep)
        * lower_x_neighbour
    )
    running_total = running_total + collide_rate * (
        (stiffness_factor + (velocity_y_grid + grid_spacing - drift_velocity_y) * half_timestep)
        * upper_mask
        * upper_y_neighbour
        + (stiffness_factor - (velocity_y_grid - grid_spacing - drift_velocity_y) * half_timestep)
        * lower_mask
        * lower_y_neighbour
    )
    running_total = running_total + collide_rate * (
        (stiffness_factor + (vertical_speeds + grid_spacing - drift_velocity_z) * half_timestep)
        * bordered_grid[2:]
        + (stiffness_factor - (vertical_speeds - grid_spacing - drift_velocity_z) * half_timestep)
        * bordered_grid[:-2]
    )
    return running_total / diagonal_factor


def shards(distribution, collision_rate):
    plane_count, column_count, row_count, velocity_width = distribution.shape
    half_width = velocity_width // 2
    velocity_x_grid, velocity_y_grid = velocity_columns()
    magnitude = step_ratio * jnp.abs(velocity_x_grid)
    extended = with_halo(distribution, (("space", 1),), 2, True)
    forward = beam_warming(
        distribution[..., half_width:],
        extended[:, 1 : column_count + 1, :, half_width:],
        extended[:, :column_count, :, half_width:],
        magnitude[half_width:],
    )
    backward = beam_warming(
        distribution[..., :half_width],
        extended[:, 3 : column_count + 3, :, :half_width],
        extended[:, 4 : column_count + 4, :, :half_width],
        magnitude[:half_width],
    )
    swept_x = jnp.concatenate([backward, forward], axis=-1)
    transported = roll_transport(swept_x, velocity_y_grid, 2)
    weights = jnp.stack(
        [
            jnp.ones_like(velocity_x_grid),
            velocity_x_grid,
            velocity_y_grid,
            velocity_x_grid * velocity_x_grid + velocity_y_grid * velocity_y_grid,
        ],
        axis=1,
    )
    partial_value = jnp.einsum(
        "zxyk,kw->wzxy", distribution, weights, precision=lax.Precision.HIGHEST
    )
    first_plane = lax.axis_index("vz") * plane_count
    local_speeds = grid_speeds(
        (first_plane + jnp.arange(plane_count, dtype=jnp.int32)).astype(jnp.float32)
    )
    moment_totals = lax.psum(combine_planes(partial_value, local_speeds[:, None, None]), "vz")
    cell_entries = tuple(
        (entry_array[None, :, :, None] for entry_array in cell_state(moment_totals))
    )
    grid_spacing = 2.0 * vel_max / V
    pointwise_rate = collision_rate[None, :, :, None]
    collide_rate = collision_scale * pointwise_rate
    relaxation_rate = relax_scale * pointwise_rate
    stiffness_factor = cell_entries[4] / (grid_spacing * grid_spacing)
    diagonal_factor = 1.0 + relaxation_rate + 6.0 * collide_rate * stiffness_factor
    index_y = jnp.arange(velocity_width, dtype=jnp.int32) % V
    upper_mask = (index_y < V - 1).astype(jnp.float32)
    lower_mask = (index_y > 0).astype(jnp.float32)
    deep_planes = with_halo(transported, (("vz", 0),), SWEEPS, False)
    plane_ids = first_plane - SWEEPS + jnp.arange(plane_count + 2 * SWEEPS, dtype=jnp.int32)
    deep_speeds = grid_speeds(plane_ids.astype(jnp.float32))[:, None, None, None]
    inside = ((plane_ids >= 0) & (plane_ids < V)).astype(jnp.float32)[:, None, None, None]
    forcing_term = deep_planes + relaxation_rate * maxwellian(
        cell_entries, velocity_x_grid, velocity_y_grid, deep_speeds
    )
    current_guess = deep_planes
    for sweep_id in range(SWEEPS):
        low_plane = sweep_id + 1
        high_plane = plane_count + 2 * SWEEPS - sweep_id - 1
        current_guess = (
            relaxation_pass(
                current_guess,
                forcing_term[low_plane:high_plane],
                diagonal_factor,
                deep_speeds[low_plane:high_plane],
                cell_entries,
                collide_rate,
                velocity_x_grid,
                velocity_y_grid,
                upper_mask,
                lower_mask,
            )
            * inside[low_plane:high_plane]
        )
    return current_guess


def solution(mesh):
    return jax.shard_map(
        shards,
        mesh=mesh,
        in_specs=(P("vz", "space", None, None), P("space", None)),
        out_specs=P("vz", "space", None, None),
        check_vma=False,
    )
```

profile of v0, /device:TPU:0, one launch (start us, length us, event | category | flops | bytes accessed | tf_op | source)
XLA Modules:
  0.0 80.3 jit_solution(2609226800865827275)
XLA Ops:
  0.0 3.4 %collective-permute-start = (f32[12,2,8,2304]{3,2,1,0:T(8,128)}, f32[12,2,8,2304]{3,2,1,0:T(8,128)S(1)}, u32[]{:S(2)}, u32[]{:S(2)}) collective-permute-start(f32[12,2,8,2304]{3,2,1,0:T(8,128)} %param.2), channel_id=1, source_target_pairs={{4,0},{8,4},{12,8},{16,12},{20,16},{24,20},{28,24},{0,28},{5,1},{9... | collective-permute-start | bytes 5308424 | tf_op jit(solution)/shard_map/ppermute | solution.py:26
  3.6 0.6 add_multiply_fusion.2
  4.2 0.6 slice_add_fusion.6
  4.8 0.7 slice_add_fusion.4
  5.5 0.6 broadcast_compare_fusion
  6.3 0.5 copy-done.1
  6.8 10.0 %fusion.6 = f32[4,12,2,8]{1,0,3,2:T(4,128)S(1)} fusion(f32[12,2,8,2304]{3,2,1,0:T(8,128)} %param.2, f32[2304,1]{0,1:T(1,128)S(1)} %multiply_add_fusion.9, f32[2304,1]{0,1:T(1,128)} %copy-done.2, f32[2304,1]{0,1:T(1,128)} %copy-done.3, f32[4]{0:T(128)S(1)} %pad.12.clone), kind=kOutput, calls=%fused_computation.28 | convolution fusion | flops 21261312 | bytes 1800208 | tf_op jit(solution)/shard_map/zxyk,kw->wzxy/dot_general | solution.py:193
  16.8 1.2 %slice_reduce_fusion = (f32[2,8]{1,0:T(2,128)S(1)}, f32[2,8]{1,0:T(2,128)}, f32[1,12,2,8]{1,0,3,2:T(1,128)}, f32[1,12,2,8]{1,0,3,2:T(1,128)}) fusion(f32[4,12,2,8]{1,0,3,2:T(4,128)S(1)} %fusion.6), kind=kLoop, calls=%fused_computation.100 | loop fusion | flops 352 | bytes 4736 | tf_op jit(solution)/shard_map/reduce_sum | solution.py:65
  18.0 1.4 %reduce_sum.45 = f32[2,8]{1,0:T(2,128)} reduce(f32[1,12,2,8]{1,3,2,0:T(8,128)} %bitcast.38, f32[]{:T(128)} %constant.47.clone.1), dimensions={0,1}, to_apply=%region_0.1 | reduce | flops 176 | bytes 836 | tf_op jit(solution)/shard_map/reduce_sum | solution.py:63
  19.4 1.3 %constant_dynamic-update-slice_fusion.4 = f32[5,2,8]{2,1,0:T(2,128)} fusion(f32[2,8]{1,0:T(2,128)} %reduce_sum.45), kind=kLoop, calls=%fused_computation.97 | loop fusion | bytes 1088
  20.7 1.2 %constant_dynamic-update-slice_fusion.3 = f32[5,2,8]{2,1,0:T(2,128)} fusion(f32[5,2,8]{2,1,0:T(2,128)} %constant_dynamic-update-slice_fusion.4, f32[2,8]{1,0:T(2,128)} %get-tuple-element.6), kind=kLoop, calls=%fused_computation.96 | loop fusion | bytes 2048
  21.9 0.6 constant_dynamic-update-slice_fusion.2
  22.5 0.8 %add_reduce_fusion = (f32[2,8]{1,0:T(2,128)S(1)}, f32[2,8]{1,0:T(2,128)S(1)}) fusion(f32[12,2,8]{0,2,1:T(8,128)} %bitcast.40, f32[12,2,8]{0,2,1:T(8,128)} %bitcast.39, f32[12]{0:T(128)} %get-tuple-element.78, f32[12]{0:T(128)} %get-tuple-element.77), kind=kLoop, calls=%fused_computation.102 | loop fusion | flops 928 | bytes 1760 | tf_op jit(solution)/shard_map/reduce_sum | solution.py:67
  23.3 0.6 constant_dynamic-update-slice_fusion.1
  23.9 0.6 constant_dynamic-update-slice_fusion
  24.5 12.8 %psum.7 = f32[5,2,8]{2,1,0:T(2,128)} all-reduce(f32[5,2,8]{2,1,0:T(2,128)} %constant_dynamic-update-slice_fusion), channel_id=1, replica_groups=mesh['space'=8,'vz'=4] {'vz'}, use_global_device_ids=true, to_apply=%region_5.6 | all-reduce | flops 80 | bytes 640 | tf_op jit(solution)/shard_map/psum | solution.py:200
  37.3 1.3 %broadcast_multiply_fusion = (f32[2,8]{1,0:T(2,128)S(1)}, f32[2,8]{1,0:T(2,128)S(1)}, f32[2,8]{1,0:T(2,128)}, f32[2,8]{1,0:T(2,128)}, f32[2,8]{1,0:T(2,128)S(1)}) fusion(f32[5,2,8]{2,1,0:T(2,128)} %psum.7), kind=kLoop, calls=%fused_computation.126 | loop fusion | flops 176 | bytes 640 | tf_op jit(solution)/shard_map/div | solution.py:135
  38.6 1.3 %subtract_multiply_fusion.1 = f32[18,2,8]{2,1,0:T(2,128)} fusion(f32[2,8]{1,0:T(2,128)S(1)} %get-tuple-element.13, f32[18]{0:T(128)} %copy-done.15), kind=kLoop, calls=%fused_computation.76 | loop fusion | flops 576 | bytes 1288 | tf_op jit(solution)/shard_map/integer_pow | solution.py:100
  39.8 1.3 %broadcast_multiply_fusion.1 = (f32[2,8]{1,0:T(2,128)}, f32[2,8]{1,0:T(2,128)}, f32[2,8]{1,0:T(2,128)}, f32[2,8]{1,0:T(2,128)}, f32[2,8]{1,0:T(2,128)}) fusion(f32[2,8]{1,0:T(2,128)} %param.3, f32[2,8]{1,0:T(2,128)S(1)} %get-tuple-element.10, f32[5,2,8]{2,1,0:T(2,128)} %psum.7), kind=kLoop, calls=%fused_computation.127 | loop fusion | flops 176 | bytes 512 | tf_op jit(solution)/shard_map/mul | solution.py:206
  41.1 1.4 %multiply_add_fusion.8 = (f32[12,2,8]{2,1,0:T(2,128)}, f32[12,2,8]{2,1,0:T(2,128)}) fusion(f32[2,8]{1,0:T(2,128)S(1)} %get-tuple-element.13, f32[2,8]{1,0:T(2,128)S(1)} %get-tuple-element.9, f32[12]{0:T(128)} %get-tuple-element.71, f32[12]{0:T(128)} %get-tuple-element.72), kind=kLoop, calls=%fused_computation.82 | loop fusion | flops 1152 | bytes 1760 | tf_op jit(solution)/shard_map/add | solution.py:156
  42.5 0.6 and_convert_fusion
  43.1 1.4 %reshape.396 = f32[2304]{0:T(1024)} reshape(f32[48,48]{1,0:T(8,128)} %copy-done.1) | data formatting | bytes 18432 | tf_op jit(solution)/shard_map/reshape | solution.py:37
  44.5 0.7 slice.234
  45.3 0.7 slice.242
  46.0 0.7 slice.250
  46.8 0.7 multiply_add_fusion.7
  47.5 0.7 broadcast_add_fusion.3
  48.3 0.9 %multiply_add_fusion.4 = (f32[2,8,2304]{2,1,0:T(8,128)S(1)}, f32[2,8,2304]{2,1,0:T(8,128)S(1)}, f32[2,8,2304]{2,1,0:T(8,128)S(1)}, f32[2,8,2304]{2,1,0:T(8,128)S(1)}, f32[2,8,2304]{2,1,0:T(8,128)S(1)}) fusion(f32[2304]{0:T(1024)S(1)} %get-tuple-element.42, f32[2,8]{1,0:T(2,128)S(1)} %get-tuple-element.9, f32[2,8]{1,0:T(2,128)} %get-tuple-element.11, ...), kind=kLoop, calls=%fused_computation.66 | loop fusion | flops 700416 | bytes 811200 | tf_op jit(solution)/shard_map/add | solution.py:142
  49.2 2.0 %multiply_add_fusion.2 = (f32[12,2,8,1152]{3,2,1,0:T(8,128)S(1)}, f32[12,2,8,1152]{3,2,1,0:T(8,128)S(1)}) fusion(f32[12,2,8,2304]{3,2,1,0:T(8,128)} %collective-permute-done.1, f32[12,2,8,2304]{3,2,1,0:T(8,128)S(1)} %copy-done, f32[1152]{0:T(1024)S(1)} %get-tuple-element.51, f32[1152]{0:T(1024)S(1)} %get-tuple-element.49, f32[1152]{0:T(1024)S(1)} %get-tuple-element.50, ...), kind=kLoop, calls=%fused_computation.57 | loop fusion | flops 5308416 | bytes 10649600 | tf_op jit(solution)/shard_map/add | solution.py:42
  51.2 0.4 fusion.14
  51.8 0.4 fusion.16
  52.2 0.3 fusion.24
  52.4 0.4 copy-done.11
  52.8 2.0 %multiply_add_fusion.1 = f32[12,2,8,2304]{3,2,1,0:T(8,128)S(1)} fusion(f32[12,2,2,2304]{3,2,1,0:T(2,128)S(1)} %get-tuple-element.35, f32[12,2,6,2304]{3,2,1,0:T(8,128)S(1)} %get-tuple-element.37, f32[12,2,6,2304]{3,2,1,0:T(8,128)S(1)} %get-tuple-element.36, f32[12,2,2,2304]{3,2,1,0:T(2,128)S(1)} %get-tuple-element.34, ...), kind=kLoop, calls=%fused_computation.54 | loop fusion | flops 7962624 | bytes 10637568 | tf_op jit(solution)/shard_map/add | solution.py:42
  55.0 1.3 %collective-permute-start.2 = (f32[3,2,8,2304]{3,2,1,0:T(8,128)S(1)}, f32[3,2,8,2304]{3,2,1,0:T(8,128)S(1)}, u32[]{:S(2)}, u32[]{:S(2)}) collective-permute-start(f32[3,2,8,2304]{3,2,1,0:T(8,128)S(1)} %get-tuple-element.28), channel_id=1, source_target_pairs={{0,1},{1,2},{2,3},{4,5},{5,6},{6,7},{8,9},{9,10},{10,11},{12,13},{... | collective-permute-start | bytes 1327112 | tf_op jit(solution)/shard_map/ppermute | solution.py:23
  56.3 1.5 %collective-permute-start.3 = (f32[3,2,8,2304]{3,2,1,0:T(8,128)S(1)}, f32[3,2,8,2304]{3,2,1,0:T(8,128)S(1)}, u32[]{:S(2)}, u32[]{:S(2)}) collective-permute-start(f32[3,2,8,2304]{3,2,1,0:T(8,128)S(1)} %get-tuple-element.29), channel_id=1, source_target_pairs={{1,0},{2,1},{3,2},{5,4},{6,5},{7,6},{9,8},{10,9},{11,10},{13,12},{... | collective-permute-start | bytes 1327112 | tf_op jit(solution)/shard_map/ppermute | solution.py:26
  58.0 5.8 %collective-permute-done.2 = f32[3,2,8,2304]{3,2,1,0:T(8,128)S(1)} collective-permute-done((f32[3,2,8,2304]{3,2,1,0:T(8,128)S(1)}, f32[3,2,8,2304]{3,2,1,0:T(8,128)S(1)}, u32[]{:S(2)}, u32[]{:S(2)}) %collective-permute-start.2) | collective-permute-done | bytes 442400 | tf_op jit(solution)/shard_map/ppermute | solution.py:23
  63.8 4.1 %collective-permute-done.3 = f32[3,2,8,2304]{3,2,1,0:T(8,128)S(1)} collective-permute-done((f32[3,2,8,2304]{3,2,1,0:T(8,128)S(1)}, f32[3,2,8,2304]{3,2,1,0:T(8,128)S(1)}, u32[]{:S(2)}, u32[]{:S(2)}) %collective-permute-start.3) | collective-permute-done | bytes 442400 | tf_op jit(solution)/shard_map/ppermute | solution.py:26
  68.0 0.8 multiply_add_fusion
  68.8 0.8 %fusion.52 = (f32[16,2,8,2256]{3,2,1,0:T(8,128)S(1)}, f32[16,2,8,2256]{3,2,1,0:T(8,128)S(1)}) fusion(f32[18,2,8,2304]{3,2,1,0:T(8,128)S(1)} %get-tuple-element.19), kind=kLoop, calls=%fused_computation.142 | loop fusion | bytes 9240576 | tf_op jit(solution)/shard_map/slice | solution.py:112
  69.6 0.8 %fusion.53 = (f32[16,2,8,2303]{3,2,1,0:T(8,128)S(1)}, f32[16,2,8,2303]{3,2,1,0:T(8,128)S(1)}) fusion(f32[18,2,8,2304]{3,2,1,0:T(8,128)S(1)} %get-tuple-element.19), kind=kLoop, calls=%fused_computation.143 | loop fusion | bytes 9433088 | tf_op jit(solution)/shard_map/slice | solution.py:114
  70.5 2.2 %fusion.4 = f32[16,2,8,2304]{3,2,1,0:T(8,128)S(1)} fusion(f32[18,2,8,2304]{3,2,1,0:T(8,128)S(1)} %get-tuple-element.19, f32[18,2,8,2304]{3,2,1,0:T(8,128)S(1)} %get-tuple-element.18, f32[16,2,8,2303]{3,2,1,0:T(8,128)S(1)} %get-tuple-element.17, f32[16,2,8,2303]{3,2,1,0:T(8,128)S(1)} %get-tuple-element.16, f32[16,2,8,2256]{3,2,1,0:T(8,128)S(1)} %get-tuple-element.15, ...), kind=kLoop, calls=%fused_computation.24 | loop fusion | flops 10027008 | bytes 19366080 | tf_op jit(solution)/shard_map/mul | solution.py:225
  72.7 0.7 fusion.54
  73.4 0.7 fusion.55
  74.2 2.1 %fusion.12 = f32[14,2,8,2304]{3,2,1,0:T(8,128)S(1)} fusion(f32[16,2,8,2304]{3,2,1,0:T(8,128)S(1)} %fusion.4, f32[18,2,8,2304]{3,2,1,0:T(8,128)S(1)} %get-tuple-element.18, f32[14,2,8,2303]{3,2,1,0:T(8,128)S(1)} %get-tuple-element.23, f32[14,2,8,2303]{3,2,1,0:T(8,128)S(1)} %get-tuple-element.22, f32[14,2,8,2256]{3,2,1,0:T(8,128)S(1)} %get-tuple-element.21, ...), kind=kLoop, calls=%fused_computation.35 | loop fusion | flops 8773632 | bytes 17019064 | tf_op jit(solution)/shard_map/mul | solution.py:225
  76.3 0.6 fusion.56
  76.9 0.6 fusion.57
  77.6 2.7 %fusion.22 = f32[12,2,8,2304]{3,2,1,0:T(8,128)} fusion(f32[14,2,8,2304]{3,2,1,0:T(8,128)S(1)} %fusion.12, f32[18,2,8,2304]{3,2,1,0:T(8,128)S(1)} %get-tuple-element.18, f32[12,2,8,2303]{3,2,1,0:T(8,128)S(1)} %get-tuple-element.27, f32[12,2,8,2303]{3,2,1,0:T(8,128)S(1)} %get-tuple-element.26, f32[12,2,8,2256]{3,2,1,0:T(8,128)S(1)} %get-tuple-element.25, ...), kind=kLoop, calls=%fused_computation.48 | loop fusion | flops 7520256 | bytes 14672048 | tf_op jit(solution)/shard_map/mul | solution.py:225
  (51 shorter events, 1.1 us)
Async XLA Ops:
  0.0 49.2 %collective-permute-start = (f32[12,2,8,2304]{3,2,1,0:T(8,128)}, f32[12,2,8,2304]{3,2,1,0:T(8,128)S(1)}, u32[]{:S(2)}, u32[]{:S(2)}) collective-permute-start(f32[12,2,8,2304]{3,2,1,0:T(8,128)} %param.2), channel_id=1, source_target_pairs={{4,0},{8,4},{12,8},{16,12},{20,16},{24,20},{28,24},{0,28},{5,1},{9... | collective-permute-start | bytes 5308424 | tf_op jit(solution)/shard_map/ppermute | solution.py:26
  3.4 45.8 %collective-permute-start.1 = (f32[12,2,8,2304]{3,2,1,0:T(8,128)}, f32[12,2,8,2304]{3,2,1,0:T(8,128)}, u32[]{:S(2)}, u32[]{:S(2)}) collective-permute-start(f32[12,2,8,2304]{3,2,1,0:T(8,128)} %param.2), channel_id=1, source_target_pairs={{0,4},{4,8},{8,12},{12,16},{16,20},{20,24},{24,28},{28,0},{1,5},{5... | collective-permute-start | bytes 5308424 | tf_op jit(solution)/shard_map/ppermute | solution.py:23
  3.6 2.7 %copy-start.2 = (f32[2304,1]{0,1:T(1,128)}, f32[2304,1]{0,1:T(1,128)S(1)}, u32[]{:S(2)}) copy-start(f32[2304,1]{0,1:T(1,128)S(1)} %stack_tile.5) | copy-start | bytes 27652
  4.2 1.3 %copy-start.15 = (f32[18]{0:T(128)}, f32[18]{0:T(128)S(1)}, u32[]{:S(2)}) copy-start(f32[18]{0:T(128)S(1)} %add_multiply_fusion.1) | copy-start | bytes 220
  6.1 0.6 copy-start.1
  6.2 0.6 copy-start.3
  6.8 42.4 %copy-start = (f32[12,2,8,2304]{3,2,1,0:T(8,128)S(1)}, f32[12,2,8,2304]{3,2,1,0:T(8,128)}, u32[]{:S(2)}) copy-start(f32[12,2,8,2304]{3,2,1,0:T(8,128)} %param.2) | copy-start | bytes 5308420
  38.6 2.6 %copy-start.7 = (f32[2,8]{1,0:T(2,128)}, f32[2,8]{1,0:T(2,128)S(1)}, u32[]{:S(2)}) copy-start(f32[2,8]{1,0:T(2,128)S(1)} %get-tuple-element.13) | copy-start | bytes 196
  52.2 0.7 copy-start.11
  54.9 2.9 %copy-start.16 = (f32[18]{0:T(128)S(1)}, f32[18]{0:T(128)}, u32[]{:S(2)}) copy-start(f32[18]{0:T(128)} %copy-done.15) | copy-start | bytes 220
  54.9 3.0 %copy-start.8 = (f32[2,8]{1,0:T(2,128)S(1)}, f32[2,8]{1,0:T(2,128)}, u32[]{:S(2)}) copy-start(f32[2,8]{1,0:T(2,128)} %copy-done.7) | copy-start | bytes 196
  54.9 13.1 %copy-start.4 = (f32[18,2,8]{2,1,0:T(2,128)S(1)}, f32[18,2,8]{2,1,0:T(2,128)}, u32[]{:S(2)}) copy-start(f32[18,2,8]{2,1,0:T(2,128)} %subtract_multiply_fusion.1) | copy-start | bytes 3460
  54.9 13.1 %copy-start.12 = (f32[2,8]{1,0:T(2,128)S(1)}, f32[2,8]{1,0:T(2,128)}, u32[]{:S(2)}) copy-start(f32[2,8]{1,0:T(2,128)} %get-tuple-element.64) | copy-start | bytes 196
  54.9 13.0 %copy-start.13 = (f32[2,8]{1,0:T(2,128)S(1)}, f32[2,8]{1,0:T(2,128)}, u32[]{:S(2)}) copy-start(f32[2,8]{1,0:T(2,128)} %get-tuple-element.66) | copy-start | bytes 196
  54.9 13.0 %copy-start.14 = (f32[2,8]{1,0:T(2,128)S(1)}, f32[2,8]{1,0:T(2,128)}, u32[]{:S(2)}) copy-start(f32[2,8]{1,0:T(2,128)} %get-tuple-element.67) | copy-start | bytes 196
  55.0 8.8 %collective-permute-start.2 = (f32[3,2,8,2304]{3,2,1,0:T(8,128)S(1)}, f32[3,2,8,2304]{3,2,1,0:T(8,128)S(1)}, u32[]{:S(2)}, u32[]{:S(2)}) collective-permute-start(f32[3,2,8,2304]{3,2,1,0:T(8,128)S(1)} %get-tuple-element.28), channel_id=1, source_target_pairs={{0,1},{1,2},{2,3},{4,5},{5,6},{6,7},{8,9},{9,10},{10,11},{12,13},{... | collective-permute-start | bytes 1327112 | tf_op jit(solution)/shard_map/ppermute | solution.py:23
  56.3 11.6 %collective-permute-start.3 = (f32[3,2,8,2304]{3,2,1,0:T(8,128)S(1)}, f32[3,2,8,2304]{3,2,1,0:T(8,128)S(1)}, u32[]{:S(2)}, u32[]{:S(2)}) collective-permute-start(f32[3,2,8,2304]{3,2,1,0:T(8,128)S(1)} %get-tuple-element.29), channel_id=1, source_target_pairs={{1,0},{2,1},{3,2},{5,4},{6,5},{7,6},{9,8},{10,9},{11,10},{13,12},{... | collective-permute-start | bytes 1327112 | tf_op jit(solution)/shard_map/ppermute | solution.py:26
  69.6 0.9 %copy-start.9 = (f32[2,8]{1,0:T(2,128)S(1)}, f32[2,8]{1,0:T(2,128)}, u32[]{:S(2)}) copy-start(f32[2,8]{1,0:T(2,128)} %get-tuple-element.63) | copy-start | bytes 196
  69.6 0.9 %copy-start.10 = (f32[2,8]{1,0:T(2,128)S(1)}, f32[2,8]{1,0:T(2,128)}, u32[]{:S(2)}) copy-start(f32[2,8]{1,0:T(2,128)} %get-tuple-element.65) | copy-start | bytes 196
  76.9 0.7 copy-start.5
  76.9 0.7 copy-start.6
where the time goes:
time: 81 us; the launch traced here: 80.3 us
  other arithmetic  27.3 us (34%)
  local copies, waits for them, and re-layouts  13.7 us (17%)
  blocking collectives  12.8 us (16%)
  matrix products  9.98 us (12%)
  waiting for transfers between devices  9.95 us (12%)
  starting transfers between devices  6.15 us (8%)
    psum x1, blocking collectives, shards(): lax.psum(combine_planes(partial_value, local_speeds[:, None, None]), 'vz')  12.8 us
    dot_general x1, matrix products, shards(): jnp.einsum('zxyk,kw->wzxy', distribution, weights, precision=lax.Precisio...  9.98 us
    mul x3, other arithmetic, shards(): relaxation_pass(current_guess, forcing_term[low_plane:high_plane], diagon...  7.04 us
    ppermute x2, waiting for transfers between devices, with_halo(): lax.ppermute(lax.slice_in_dim(block, block.shape[dim] - width, None, axis...  5.81 us
    ppermute x2, starting transfers between devices, with_halo(): lax.ppermute(lax.slice_in_dim(block, 0, width, axis=dim), axis, backward)  4.83 us
    unnamed x38, local copies, waits for them, and re-layouts  4.77 us
    ppermute x2, waiting for transfers between devices, with_halo(): lax.ppermute(lax.slice_in_dim(block, 0, width, axis=dim), axis, backward)  4.14 us
    add x2, other arithmetic, beam_warming(): middle - 0.5 * magnitude * (3.0 * middle - 4.0 * near_cells + far_cells)  3.98 us
  transfers between devices with their start and end apart: 4, of which 2 were waited for; matrix products, arithmetic and copies ran while one was open for 40% of the time, Pallas kernels for 0%

commit v1 on v0

v1 whole, which is shorter than its diff:
```python
import functools

import jax
import jax.numpy as jnp
from jax import lax
from jax.experimental import pallas as pl
from jax.experimental.pallas import tpu as pltpu
from jax.sharding import PartitionSpec as P

V = 48
SWEEPS = 3
HALO = 2
LANES = 128
MESH = pl.DeviceIdType.MESH

vel_max = 4.5
step_ratio = 0.1
collision_scale = 0.004
relax_scale = 0.5
spacing = 2.0 * vel_max / V


def grid_speeds(position):
    return vel_max * (2.0 * position + 1.0 - V) / V


def lane_speeds(first_lane, shape):
    lane = lax.broadcasted_iota(jnp.int32, shape, len(shape) - 1).astype(jnp.float32) + first_lane
    index_x = jnp.floor((lane + 0.5) * (1.0 / V))
    index_y = lane - V * index_x
    return index_x, index_y


def warming_coefficients(speed):
    a = step_ratio * jnp.abs(speed)
    return 1.0 - 1.5 * a + 0.5 * a * a, 2.0 * a - a * a, 0.5 * a * a - 0.5 * a


RDIAG, GAIN, RATE, UP_Z, DOWN_Z, MEAN_Z, HALF_T = range(7)
X0, X1, X2, Y0, Y1, Y2, POS = range(7)
UP_X, DOWN_X, UP_Y, DOWN_Y, GAUSS = range(5)


def kernel(
    space_size,
    vz_size,
    f_hbm,
    rate_hbm,
    out_ref,
    f_ref,
    rate_ref,
    low_ref,
    high_ref,
    t_ref,
    src_ref,
    g1_ref,
    g2_ref,
    lane_ref,
    coef_ref,
    par_ref,
    mom_ref,
    local_sem,
    send_sem,
    recv_sem,
    zsend_sem,
    zrecv_sem,
    msend_sem,
    mrecv_sem,
):
    planes, cols, rows, width = f_ref.shape
    half = width // 2
    tiles = width // LANES
    space = lax.axis_index("space")
    vz = lax.axis_index("vz")
    right = lax.rem(space + 1, space_size)
    left = lax.rem(space + space_size - 1, space_size)
    first_plane = vz * planes
    tile_shape = (rows, LANES)

    f_copy = pltpu.make_async_copy(f_hbm, f_ref, local_sem.at[0])
    rate_copy = pltpu.make_async_copy(rate_hbm, rate_ref, local_sem.at[1])
    f_copy.start()
    rate_copy.start()

    barrier = pltpu.get_barrier_semaphore()
    for neighbour in (left, right):
        pl.semaphore_signal(
            barrier, inc=1, device_id={"space": neighbour}, device_id_type=MESH
        )
    for step in range(1, vz_size):
        pl.semaphore_signal(
            barrier,
            inc=1,
            device_id={"vz": lax.rem(vz + step, vz_size)},
            device_id_type=MESH,
        )
    pl.semaphore_wait(barrier, 2 + vz_size - 1)

    def to_right(p):
        return pltpu.make_async_remote_copy(
            src_ref=f_hbm.at[p, pl.ds(cols - HALO, HALO), :, pl.ds(half, half)],
            dst_ref=low_ref.at[p],
            send_sem=send_sem.at[0, p],
            recv_sem=recv_sem.at[0, p],
            device_id={"space": right},
            device_id_type=MESH,
        )

    def to_left(p):
        return pltpu.make_async_remote_copy(
            src_ref=f_hbm.at[p, pl.ds(0, HALO), :, pl.ds(0, half)],
            dst_ref=high_ref.at[p],
            send_sem=send_sem.at[1, p],
            recv_sem=recv_sem.at[1, p],
            device_id={"space": left},
            device_id_type=MESH,
        )

    def z_down(j):
        return pltpu.make_async_remote_copy(
            src_ref=t_ref.at[SWEEPS + j],
            dst_ref=t_ref.at[planes + SWEEPS + j],
            send_sem=zsend_sem.at[0, j],
            recv_sem=zrecv_sem.at[0, j],
            device_id={"vz": jnp.maximum(vz - 1, 0)},
            device_id_type=MESH,
        )

    def z_up(j):
        return pltpu.make_async_remote_copy(
            src_ref=t_ref.at[planes + SWEEPS - 1 - j],
            dst_ref=t_ref.at[SWEEPS - 1 - j],
            send_sem=zsend_sem.at[1, j],
            recv_sem=zrecv_sem.at[1, j],
            device_id={"vz": jnp.minimum(vz + 1, vz_size - 1)},
            device_id_type=MESH,
        )

    @pl.loop(0, planes // 2)
    def _(i):
        for p in (i, planes - 1 - i):
            to_right(p).start()
            to_left(p).start()

    index_x, index_y = lane_speeds(0.0, (rows, width))
    speed_x, speed_y = grid_speeds(index_x), grid_speeds(index_y)
    for row, value in zip((X0, X1, X2), warming_coefficients(speed_x)):
        lane_ref[row] = value
    for row, value in zip((Y0, Y1, Y2), warming_coefficients(speed_y)):
        lane_ref[row] = value
    lane_ref[POS] = speed_y

    @pl.when(vz == 0)
    def _():
        for ref in (t_ref, g1_ref, g2_ref):
            ref[SWEEPS - 1] = jnp.zeros(ref.shape[1:], jnp.float32)

    @pl.when(vz == vz_size - 1)
    def _():
        for ref in (t_ref, g1_ref, g2_ref):
            ref[planes + SWEEPS] = jnp.zeros(ref.shape[1:], jnp.float32)

    f_copy.wait()
    plane_speeds = [grid_speeds((first_plane + p).astype(jnp.float32)) for p in range(planes)]

    def moment_tile(j, sums):
        tile_x, tile_y = lane_speeds((j * LANES).astype(jnp.float32), tile_shape)
        tile_x, tile_y = grid_speeds(tile_x), grid_speeds(tile_y)
        square = tile_x * tile_x + tile_y * tile_y
        lanes = pl.ds(pl.multiple_of(j * LANES, LANES), LANES)
        result = []
        for c in range(cols):
            total, first, second = 0.0, 0.0, 0.0
            for p in range(planes):
                value = f_ref[p, c, :, lanes]
                moved = value * plane_speeds[p]
                total = total + value
                first = first + moved
                second = second + moved * plane_speeds[p]
            m = sums[5 * c : 5 * c + 5]
            result += [
                m[0] + total,
                m[1] + total * tile_x,
                m[2] + total * tile_y,
                m[3] + first,
                m[4] + total * square + second,
            ]
        return tuple(result)

    zero = jnp.zeros(tile_shape, jnp.float32)
    sums = lax.fori_loop(0, tiles, moment_tile, (zero,) * (5 * cols))
    lane = lax.broadcasted_iota(jnp.int32, tile_shape, 1)
    packed = zero
    for j, value in enumerate(sums):
        packed = jnp.where(lane == j, jnp.sum(value, axis=1, keepdims=True), packed)
    mom_ref[0] = packed

    def moment_copy(step):
        return pltpu.make_async_remote_copy(
            src_ref=mom_ref.at[0],
            dst_ref=mom_ref.at[step],
            send_sem=msend_sem.at[step],
            recv_sem=mrecv_sem.at[step],
            device_id={"vz": lax.rem(vz + step, vz_size)},
            device_id_type=MESH,
        )

    for step in range(1, vz_size):
        moment_copy(step).start()

    def column(p, c, lanes):
        if c < 0:
            return low_ref[p, c + HALO]
        if c >= cols:
            return high_ref[p, c - cols]
        return f_ref[p, c, :, lanes]

    def transport(p):
        back, fore = slice(0, half), slice(half, width)
        for c in range(cols):
            backward = (
                lane_ref[X0, :, back] * f_ref[p, c, :, back]
                + lane_ref[X1, :, back] * column(p, c + 1, back)
                + lane_ref[X2, :, back] * column(p, c + 2, back)
            )
            forward = (
                lane_ref[X0, :, fore] * f_ref[p, c, :, fore]
                + lane_ref[X1, :, fore] * column(p, c - 1, fore)
                + lane_ref[X2, :, fore] * column(p, c - 2, fore)
            )
            for swept, lanes in ((backward, back), (forward, fore)):
                positive = lane_ref[POS, :, lanes] > 0.0
                ahead = pltpu.roll(swept, rows - 2, 0)
                near = pltpu.roll(jnp.where(positive, swept, ahead), 1, 0)
                far = jnp.where(positive, pltpu.roll(swept, 2, 0), ahead)
                t_ref[p + SWEEPS, c, :, lanes] = (
                    lane_ref[Y0, :, lanes] * swept
                    + lane_ref[Y1, :, lanes] * near
                    + lane_ref[Y2, :, lanes] * far
                )

    def pair(i):
        for p in (i, planes - 1 - i):
            to_right(p).wait_recv()
            to_left(p).wait_recv()
            transport(p)

    @pl.loop(0, SWEEPS)
    def _(i):
        pair(i)

        @pl.when(vz > 0)
        def _():
            z_down(i).start()

        @pl.when(vz < vz_size - 1)
        def _():
            z_up(i).start()

    for step in range(1, vz_size):
        moment_copy(step).wait_recv()
    packed = mom_ref[0]
    for step in range(1, vz_size):
        packed = packed + mom_ref[step]
    rate_copy.wait()
    diagonal_mask = lax.broadcasted_iota(jnp.int32, (rows, rows), 0) == lax.broadcasted_iota(
        jnp.int32, (rows, rows), 1
    )

    def spread(value):
        return jnp.concatenate([value] * tiles, axis=1)

    for c in range(cols):
        m0, m1, m2, m3, m4 = (
            jnp.broadcast_to(
                jnp.sum(jnp.where(lane == 5 * c + j, packed, 0.0), axis=1, keepdims=True),
                tile_shape,
            )
            for j in range(5)
        )
        point_rate = jnp.broadcast_to(
            jnp.sum(
                jnp.where(
                    diagonal_mask,
                    jnp.broadcast_to(rate_ref[c : c + 1, :], (rows, rows)),
                    0.0,
                ),
                axis=1,
                keepdims=True,
            ),
            tile_shape,
        )
        ux, uy, uz = m1 / m0, m2 / m0, m3 / m0
        temperature = (m4 / m0 - ux * ux - uy * uy - uz * uz) / 3.0
        density = m0 * spacing**3
        rate = collision_scale * point_rate
        relax = relax_scale * point_rate
        stiff = temperature / (spacing * spacing)
        diagonal = 1.0 + relax + 6.0 * rate * stiff
        scaled = rate / diagonal
        slope = scaled * (0.5 / spacing)
        base = scaled * (stiff + 0.5)
        width_t = 2.0 * jnp.pi * temperature
        half_t = 0.5 / temperature
        par_ref[c, RDIAG] = 1.0 / diagonal
        par_ref[c, GAIN] = relax / diagonal * density / (width_t * jnp.sqrt(width_t))
        par_ref[c, RATE] = slope
        par_ref[c, UP_Z] = base - slope * uz
        par_ref[c, DOWN_Z] = base + slope * uz
        par_ref[c, MEAN_Z] = uz
        par_ref[c, HALF_T] = half_t
        ix, iy = lane_speeds(0.0, (rows, width))
        cx, cy = grid_speeds(ix), grid_speeds(iy)
        coef_ref[c, UP_X] = jnp.where(
            ix < V - 1.5, spread(base - slope * ux) + spread(slope) * cx, 0.0
        )
        coef_ref[c, DOWN_X] = jnp.where(
            ix > 0.5, spread(base + slope * ux) - spread(slope) * cx, 0.0
        )
        coef_ref[c, UP_Y] = jnp.where(
            iy < V - 1.5, spread(base - slope * uy) + spread(slope) * cy, 0.0
        )
        coef_ref[c, DOWN_Y] = jnp.where(
            iy > 0.5, spread(base + slope * uy) - spread(slope) * cy, 0.0
        )
        off_x = cx - spread(ux)
        off_y = cy - spread(uy)
        coef_ref[c, GAUSS] = jnp.exp(-(off_x * off_x + off_y * off_y) * spread(half_t))

    def sweep(level, k):
        b = k + SWEEPS
        old = (t_ref, g1_ref, g2_ref)[level]
        cz = grid_speeds((first_plane + k).astype(jnp.float32))
        for c in range(cols):
            slope = par_ref[c, RATE]
            up_z = spread(par_ref[c, UP_Z] + slope * cz)
            down_z = spread(par_ref[c, DOWN_Z] - slope * cz)
            middle = old[b, c]
            if level == 0:
                off_z = cz - par_ref[c, MEAN_Z]
                gain = par_ref[c, GAIN] * jnp.exp(-off_z * off_z * par_ref[c, HALF_T])
                source = spread(par_ref[c, RDIAG]) * middle + spread(gain) * coef_ref[c, GAUSS]
                src_ref[b, c] = source
            else:
                source = src_ref[b, c]
            total = (
                source
                + up_z * old[b + 1, c]
                + down_z * old[b - 1, c]
                + coef_ref[c, UP_X] * pltpu.roll(middle, width - V, 1)
                + coef_ref[c, DOWN_X] * pltpu.roll(middle, V, 1)
                + coef_ref[c, UP_Y] * pltpu.roll(middle, width - 1, 1)
                + coef_ref[c, DOWN_Y] * pltpu.roll(middle, 1, 1)
            )
            if level == SWEEPS - 1:
                out_ref[k, c] = total
            else:
                (g1_ref, g2_ref)[level][b, c] = total

    def sweep_range(level, low, high):
        if low < 0:
            low = jnp.where(vz == 0, 0, low)
        if high > planes:
            high = jnp.where(vz == vz_size - 1, planes, high)

        @pl.loop(low, high)
        def _(k):
            sweep(level, k)

    last = planes // 2 - 1

    @pl.loop(SWEEPS, last)
    def _(i):
        pair(i)

    @pl.when(vz < vz_size - 1)
    def _():
        for j in range(SWEEPS):
            z_down(j).wait_recv()

    @pl.when(vz > 0)
    def _():
        for j in range(SWEEPS):
            z_up(j).wait_recv()

    for level in range(SWEEPS):
        inner = level + 1
        outer = SWEEPS - 1 - level
        sweep_range(level, -outer, last - inner)
        sweep_range(level, planes - last + inner, planes + outer)

    pair(last)
    for level in range(SWEEPS):
        inner = level + 1
        sweep_range(level, last - inner, planes - last + inner)

    @pl.loop(0, planes)
    def _(p):
        to_right(p).wait_send()
        to_left(p).wait_send()

    for step in range(1, vz_size):
        moment_copy(step).wait_send()

    @pl.when(vz > 0)
    def _():
        for j in range(SWEEPS):
            z_down(j).wait_send()

    @pl.when(vz < vz_size - 1)
    def _():
        for j in range(SWEEPS):
            z_up(j).wait_send()


def solution(mesh):
    space_size, vz_size = mesh.shape["space"], mesh.shape["vz"]

    def shards(distribution, collision_rate):
        planes, cols, rows, width = distribution.shape
        f32 = jnp.float32
        deep = (planes + 2 * SWEEPS, cols, rows, width)
        halo = (planes, HALO, rows, width // 2)
        dma = pltpu.SemaphoreType.DMA
        return pl.pallas_call(
            functools.partial(kernel, space_size, vz_size),
            out_shape=jax.ShapeDtypeStruct(distribution.shape, f32),
            in_specs=[pl.BlockSpec(memory_space=pl.ANY)] * 2,
            out_specs=pl.BlockSpec(memory_space=pltpu.VMEM),
            scratch_shapes=[
                pltpu.VMEM(distribution.shape, f32),
                pltpu.VMEM(collision_rate.shape, f32),
                pltpu.VMEM(halo, f32),
                pltpu.VMEM(halo, f32),
                pltpu.VMEM(deep, f32),
                pltpu.VMEM(deep, f32),
                pltpu.VMEM(deep, f32),
                pltpu.VMEM(deep, f32),
                pltpu.VMEM((7, rows, width), f32),
                pltpu.VMEM((cols, 5, rows, width), f32),
                pltpu.VMEM((cols, 7, rows, LANES), f32),
                pltpu.VMEM((vz_size, rows, LANES), f32),
                dma((2,)),
                dma((2, planes)),
                dma((2, planes)),
                dma((2, SWEEPS)),
                dma((2, SWEEPS)),
                dma((vz_size,)),
                dma((vz_size,)),
            ],
            compiler_params=pltpu.CompilerParams(
                collective_id=0, has_side_effects=True, vmem_limit_bytes=40 * 1024 * 1024
            ),
            name="transport_and_relax",
        )(distribution, collision_rate)

    return jax.shard_map(
        shards,
        mesh=mesh,
        in_specs=(P("vz", "space", None, None), P("space", None)),
        out_specs=P("vz", "space", None, None),
        check_vma=False,
    )
```

time: 81 us -> 37.1 us (0.46)
  the two profiles are of different devices: /device:TPU:0 before, /device:TPU:1 now
where the time goes in v1:
time: 37.1 us; the launch traced here: 37 us
  Pallas kernels  33.6 us (91%)
  local copies, waits for them, and re-layouts  3.36 us (9%)
    pallas_call x1, Pallas kernels, shards(): pl.pallas_call(functools.partial(kernel, space_size, vz_size), out_shape=...  33.6 us
    unnamed x5, local copies, waits for them, and re-layouts  3.36 us

profile of v1, /device:TPU:1, one launch (start us, length us, event | category | flops | bytes accessed | tf_op | source)
XLA Modules:
  0.0 37.0 jit_solution(8304597635323214304)
XLA Ops:
  0.0 0.0 copy-start
  0.0 1.5 %copy-done = f32[12,2,8,2304]{3,2,1,0:T(8,128)S(1)} copy-done((f32[12,2,8,2304]{3,2,1,0:T(8,128)S(1)}, f32[12,2,8,2304]{3,2,1,0:T(8,128)}, u32[]{:S(2)}) %copy-start) | copy-done | bytes 1769496
  1.5 0.0 copy-start.1
  1.5 0.7 %copy-done.1 = f32[2,8]{1,0:T(2,128)S(1)} copy-done((f32[2,8]{1,0:T(2,128)S(1)}, f32[2,8]{1,0:T(2,128)}, u32[]{:S(2)}) %copy-start.1) | copy-done | bytes 88
  2.2 33.6 %transport_and_relax.1 = f32[12,2,8,2304]{3,2,1,0:T(8,128)S(1)} custom-call(f32[12,2,8,2304]{3,2,1,0:T(8,128)S(1)} %copy-done, f32[2,8]{1,0:T(2,128)S(1)} %copy-done.1), custom_call_target="tpu_custom_call" | custom-call | tf_op jit(solution)/shard_map/transport_and_relax/pallas_call | solution.py:425
  35.8 1.2 %copy.4 = f32[12,2,8,2304]{3,2,1,0:T(8,128)} copy(f32[12,2,8,2304]{3,2,1,0:T(8,128)S(1)} %transport_and_relax.1) | data formatting | bytes 3538944
Async XLA Ops:
  0.0 1.5 %copy-start = (f32[12,2,8,2304]{3,2,1,0:T(8,128)S(1)}, f32[12,2,8,2304]{3,2,1,0:T(8,128)}, u32[]{:S(2)}) copy-start(f32[12,2,8,2304]{3,2,1,0:T(8,128)} %f_hbm.1) | copy-start | bytes 5308420
  1.5 0.7 %copy-start.1 = (f32[2,8]{1,0:T(2,128)S(1)}, f32[2,8]{1,0:T(2,128)}, u32[]{:S(2)}) copy-start(f32[2,8]{1,0:T(2,128)} %rate_hbm.1) | copy-start | bytes 196

commit v2 on v1

--- a/solution.py
+++ b/solution.py
@@ -239,19 +239,20 @@
                     + lane_ref[Y2, :, lanes] * far
                 )
 
-    def pair(i):
-        for p in (i, planes - 1 - i):
-            to_right(p).wait_recv()
-            to_left(p).wait_recv()
-            transport(p)
+    def arrive(p):
+        to_right(p).wait_recv()
+        to_left(p).wait_recv()
+        transport(p)
 
     @pl.loop(0, SWEEPS)
     def _(i):
-        pair(i)
+        arrive(i)
 
         @pl.when(vz > 0)
         def _():
             z_down(i).start()
+
+        arrive(planes - 1 - i)
 
         @pl.when(vz < vz_size - 1)
         def _():
@@ -357,42 +358,56 @@
             else:
                 (g1_ref, g2_ref)[level][b, c] = total
 
-    def sweep_range(level, low, high):
-        if low < 0:
-            low = jnp.where(vz == 0, 0, low)
-        if high > planes:
-            high = jnp.where(vz == vz_size - 1, planes, high)
-
-        @pl.loop(low, high)
+    def sweep_both(level, items):
+        step = items[1] - items[0] if len(items) > 1 else 0
+
+        @pl.loop(0, 2 * len(items))
+        def _(n):
+            near = items[0] + step * (n // 2)
+            far_side = n % 2
+            k = near + far_side * (planes - 1 - 2 * near)
+            plane = first_plane + k
+
+            @pl.when((plane >= 0) & (plane < planes * vz_size))
+            def _():
+                sweep(level, k)
+
+    def wait_halo(j):
+        @pl.when(vz < vz_size - 1)
+        def _():
+            z_down(j).wait_recv()
+
+        @pl.when(vz > 0)
+        def _():
+            z_up(j).wait_recv()
+
+    last = planes // 2 - 1
+    done = [(0, 0)] * SWEEPS
+    for i in range(SWEEPS - 1, last):
+        if i >= SWEEPS:
+            arrive(i)
+            arrive(planes - 1 - i)
+        halos = min(i - SWEEPS + 2, SWEEPS)
+        if i - SWEEPS + 1 < SWEEPS:
+            wait_halo(i - SWEEPS + 1)
+        for level in range(SWEEPS):
+            low, high = level + 1 - halos, i - level
+            if low < high:
+                old_low, old_high = done[level] if done[level][1] > done[level][0] else (low, low)
+                items = [*range(low, old_low), *range(old_high, high)]
+                for first in range(0, len(items), 2):
+                    sweep_both(level, items[first : first + 2])
+                done[level] = (low, high)
+
+    arrive(last)
+    for level in range(SWEEPS):
+        sweep(level, last - 1 - level)
+    arrive(planes - 1 - last)
+    for level in range(SWEEPS):
+
+        @pl.loop(last - level, planes - last + level + 1)
         def _(k):
             sweep(level, k)
-
-    last = planes // 2 - 1
-
-    @pl.loop(SWEEPS, last)
-    def _(i):
-        pair(i)
-
-    @pl.when(vz < vz_size - 1)
-    def _():
-        for j in range(SWEEPS):
-            z_down(j).wait_recv()
-
-    @pl.when(vz > 0)
-    def _():
-        for j in range(SWEEPS):
-            z_up(j).wait_recv()
-
-    for level in range(SWEEPS):
-        inner = level + 1
-        outer = SWEEPS - 1 - level
-        sweep_range(level, -outer, last - inner)
-        sweep_range(level, planes - last + inner, planes + outer)
-
-    pair(last)
-    for level in range(SWEEPS):
-        inner = level + 1
-        sweep_range(level, last - inner, planes - last + inner)
 
     @pl.loop(0, planes)
     def _(p):
@@ -452,7 +467,7 @@
                 collective_id=0, has_side_effects=True, vmem_limit_bytes=40 * 1024 * 1024
             ),
             name="transport_and_relax",
-        )(distribution, collision_rate)
+        )(*(pltpu.with_memory_space_constraint(x, pltpu.HBM) for x in (distribution, collision_rate)))
 
     return jax.shard_map(
         shards,

time: 37.1 us -> 32.3 us (0.87)
  Pallas kernels: 33.6 us -> 30.9 us
  local copies, waits for them, and re-layouts: 3.36 us -> 1.21 us
    pallas_call x1, Pallas kernels: 33.6 us -> 30.9 us  [shards(): pl.pallas_call(functools.partial(kernel, space_size, vz_size), out_shape=...]
    unnamed x5 -> x1, local copies, waits for them, and re-layouts: 3.36 us -> 1.21 us
where the time goes in v2:
time: 32.3 us; the launch traced here: 32.1 us
  Pallas kernels  30.9 us (96%)
  local copies, waits for them, and re-layouts  1.21 us (4%)
    pallas_call x1, Pallas kernels, shards(): pl.pallas_call(functools.partial(kernel, space_size, vz_size), out_shape=...  30.9 us
    unnamed x1, local copies, waits for them, and re-layouts  1.21 us

profile of v2, /device:TPU:1, one launch (start us, length us, event | category | flops | bytes accessed | tf_op | source)
XLA Modules:
  0.0 32.1 jit_solution(7141114940313287962)
XLA Ops:
  0.0 30.9 %transport_and_relax.1 = f32[12,2,8,2304]{3,2,1,0:T(8,128)S(1)} custom-call(f32[12,2,8,2304]{3,2,1,0:T(8,128)} %f_hbm.1, f32[2,8]{1,0:T(2,128)} %rate_hbm.1), custom_call_target="tpu_custom_call" | custom-call | tf_op jit(solution)/shard_map/transport_and_relax/pallas_call | solution.py:440
  30.9 1.2 %copy.4 = f32[12,2,8,2304]{3,2,1,0:T(8,128)} copy(f32[12,2,8,2304]{3,2,1,0:T(8,128)S(1)} %transport_and_relax.1) | data formatting | bytes 3538944
